TPU v7x, 32 devices: a whole 2x2x4 slice. The times are simulated.
32 devices in a mesh: tm: 16 (over z, x, core), space: 2 (over y).
Axes of the slice: x: 2, y: 2, z: 4, core: 2. Of those that a mesh axis runs over, the one named last changes fastest.
Arguments:
- snapshots: bfloat16 [512, 5, 4096], P('tm', None, 'space'), may hold values from -210 to 210, as said below
- basis: bfloat16 [2, 33, 16, 5, 4096], P(None, None, None, None, ('space', 'tm')), may hold values from -6 to 6
- mass_table: float32 [8, 64, 64], replicated, may hold values from -0.03 to 3, as said below
- elem_kind: int32 [64], P(('space', 'tm')), may hold values from 0 to 7
- offsets: int32 [8], replicated, may hold values from 0 to 256, as said below
Outputs:
- coeffs: float32 [2, 33, 8, 16], replicated
- new_basis: bfloat16 [2, 33, 16, 5, 4096], P(None, None, None, None, ('space', 'tm'))
Inputs may be any that keep to these rules, and one draw needn't show every extreme that they name: `snapshots`: rows of flow data. `mass_table`: each block is symmetric and positive definite. `offsets`: some block starts at 0 and some at 256.
All inputs are finite; a program needn't handle non-finite values.
Results may differ from a plain program's by a relative error of at most 0.0095.
Values may be sent and summed in bfloat16 or wider, within the bound.
A program may use at most 64 MiB of HBM per device.

v0:
```python
import math

import jax
import jax.numpy as jnp
from jax import lax
from jax.sharding import PartitionSpec as P

NT = 256


def spectral_table(offsets, window_len, freq_count, record_len):
    snap_idx = jnp.arange(record_len, dtype=jnp.int32)
    time_lag = snap_idx[None, :] - offsets[:, None]
    inside = (time_lag >= 0) & (time_lag < window_len)
    lag_clip = jnp.clip(time_lag, 0, window_len - 1)
    lag_float = lag_clip.astype(jnp.float32)
    hann_wt = 0.5 - 0.5 * jnp.cos(2.0 * math.pi / window_len * lag_float)
    norm_wt = 1.0 / math.sqrt(0.375 * window_len)
    freq_idx = jnp.arange(freq_count, dtype=jnp.int32)
    phase_int = jnp.mod(freq_idx[:, None, None] * lag_clip[None], window_len)
    angle = 2.0 * math.pi / window_len * phase_int.astype(jnp.float32)
    weight = jnp.where(inside, hann_wt * norm_wt, jnp.zeros_like(hann_wt))[None]
    real_part = weight * jnp.cos(angle)
    imag_part = -weight * jnp.sin(angle)
    return jnp.stack([real_part, imag_part]).astype(jnp.bfloat16)


def apply_mass(field, local_mass):
    lead = field.shape[:-1]
    elem_count = local_mass.shape[0]
    shaped = field.reshape(lead + (elem_count, local_mass.shape[1]))
    result = jnp.einsum("...ep,epq->...eq", shaped, local_mass, precision=lax.Precision.HIGHEST)
    return result.reshape(field.shape)


def paired_einsum(pattern, first_pair, second_pair):
    real_out = jnp.einsum(
        pattern, first_pair[0], second_pair[0], preferred_element_type=jnp.float32
    ) + jnp.einsum(pattern, first_pair[1], second_pair[1], preferred_element_type=jnp.float32)
    imag_out = jnp.einsum(
        pattern, first_pair[0], second_pair[1], preferred_element_type=jnp.float32
    ) - jnp.einsum(pattern, first_pair[1], second_pair[0], preferred_element_type=jnp.float32)
    return (real_out, imag_out)


def on_device(snapshots, basis, mass_table, elem_kind, offsets):
    regrouped = lax.all_to_all(snapshots, "tm", split_axis=2, concat_axis=0, tiled=True)
    record_len, var_count, local_pts = regrouped.shape
    freq_count = basis.shape[1]
    mode_count = basis.shape[2]
    block_total = offsets.shape[0]
    kind_count = mass_table.shape[0]
    flat_len = var_count * local_pts
    entries = flat_len * lax.axis_size("tm") * lax.axis_size("space")
    dft_table = spectral_table(offsets, NT, freq_count, record_len)
    record_flat = regrouped.reshape(record_len, flat_len)
    spectra = jnp.dot(
        dft_table.reshape(2 * freq_count * block_total, record_len),
        record_flat,
        preferred_element_type=jnp.float32,
    )
    selector = (elem_kind[:, None] == jnp.arange(kind_count, dtype=jnp.int32)[None, :]).astype(
        jnp.float32
    )
    local_mass = jnp.einsum("ek,kpq->epq", selector, mass_table, precision=lax.Precision.HIGHEST)
    spectra = spectra.reshape(2, freq_count, block_total, var_count, local_pts)
    weighted = (
        apply_mass(spectra, local_mass)
        .astype(jnp.bfloat16)
        .reshape(2, freq_count, block_total, flat_len)
    )
    mode_rows = basis.reshape(2, freq_count, mode_count, flat_len)
    coeff_real, coeff_imag = paired_einsum("fkx,fbx->fbk", mode_rows, weighted)
    coeff_part = jnp.stack([coeff_real, coeff_imag])
    spec_round = spectra.astype(jnp.bfloat16).reshape(2, freq_count, block_total, flat_len)
    gram_real, gram_imag = paired_einsum("fbx,fcx->fbc", spec_round, weighted)
    coeff_sum, gram_real, gram_imag = lax.psum((coeff_part, gram_real, gram_imag), ("tm", "space"))
    coeffs = coeff_sum / math.sqrt(entries)
    table_float = dft_table.astype(jnp.float32)
    coeff_round = lax.optimization_barrier(coeffs.astype(jnp.bfloat16)).astype(jnp.float32)
    kernel_real = jnp.einsum("fbt,fbk->fkt", table_float[0], coeff_round[0]) - jnp.einsum(
        "fbt,fbk->fkt", table_float[1], coeff_round[1]
    )
    kernel_imag = jnp.einsum("fbt,fbk->fkt", table_float[0], coeff_round[1]) + jnp.einsum(
        "fbt,fbk->fkt", table_float[1], coeff_round[0]
    )
    kernel = (
        jnp.stack([kernel_real, kernel_imag])
        .astype(jnp.bfloat16)
        .reshape(2 * freq_count * mode_count, record_len)
    )
    fields = jnp.dot(kernel, record_flat, preferred_element_type=jnp.float32)
    fields = fields.reshape(2, freq_count, mode_count, var_count, local_pts)
    apply_real = jnp.einsum("fbc,fck->fbk", gram_real, coeff_round[0]) - jnp.einsum(
        "fbc,fck->fbk", gram_imag, coeff_round[1]
    )
    apply_imag = jnp.einsum("fbc,fck->fbk", gram_real, coeff_round[1]) + jnp.einsum(
        "fbc,fck->fbk", gram_imag, coeff_round[0]
    )
    energy = jnp.sum(coeff_round[0] * apply_real + coeff_round[1] * apply_imag, axis=1)
    factor = 1.0 / jnp.sqrt(energy / entries + 1e-06)
    new_basis = (fields * factor[None, :, :, None, None]).astype(jnp.bfloat16)
    return (coeffs, new_basis)


def solution(mesh):
    return jax.shard_map(
        on_device,
        mesh=mesh,
        in_specs=(
            P("tm", None, "space"),
            P(None, None, None, None, ("space", "tm")),
            P(),
            P(("space", "tm")),
            P(),
        ),
        out_specs=(P(), P(None, None, None, None, ("space", "tm"))),
        check_vma=False,
    )
```

profile of v0, /device:TPU:0, one launch (start us, length us, event | category | flops | bytes accessed | tf_op | source)
XLA Modules:
  0.0 120.1 jit_solution(16826947783138899716)
XLA Ops:
  0.6 5.4 %copy.35 = bf16[32,5,2048]{0,1,2:T(8,128)(2,1)} copy(bf16[32,5,2048]{2,0,1:T(8,128)(2,1)} %param.5) | data formatting | bytes 1310720 | tf_op args[0]
  6.0 5.2 %reshape.176 = bf16[16,2,10240]{2,1,0:T(2,128)(2,1)} reshape(bf16[2048,5,32]{2,1,0:T(8,128)(2,1)} %bitcast.99) | data formatting | bytes 1310720
  11.3 7.4 %all-to-all-start = ((bf16[16,2,10240]{2,1,0:T(2,128)(2,1)}), bf16[16,2,10240]{2,1,0:T(2,128)(2,1)S(1)}, u32[]{:S(2)}, u32[]{:S(2)}) async-start(bf16[16,2,10240]{2,1,0:T(2,128)(2,1)} %reshape.176), calls=%async_computation | async-start | bytes 1310720 | tf_op jit(solution)/shard_map/all_to_all | solution.py:47
  19.2 1.6 %squeeze.25 = bf16[33,16,640]{2,1,0:T(8,128)(2,1)} reshape(bf16[1,33,16,5,128]{4,3,2,1,0:T(8,128)(2,1)S(1)} %copy.40) | data formatting | bytes 1351680 | tf_op jit(solution)/shard_map/squeeze | solution.py:38
  21.1 1.7 %squeeze.27 = bf16[33,16,640]{2,1,0:T(8,128)(2,1)} reshape(bf16[1,33,16,5,128]{4,3,2,1,0:T(8,128)(2,1)S(1)} %copy.42) | data formatting | bytes 1351680 | tf_op jit(solution)/shard_map/squeeze | solution.py:39
  22.8 0.4 convolution_bitcast_fusion
  23.4 2.2 %multiply_convert_fusion.2 = (bf16[1,33,8,512]{3,2,1,0:T(8,128)(2,1)S(1)}, bf16[1,33,8,512]{3,2,1,0:T(8,128)(2,1)S(1)}) fusion(s32[8,512]{1,0:T(8,128)S(1)} %fusion.42, f32[8,512]{1,0:T(8,128)S(1)} %get-tuple-element.21, f32[8,512]{1,0:T(8,128)S(1)} %get-tuple-element.22), kind=kLoop, calls=%fused_computation.38 | loop fusion | flops 2433024 | bytes 589824 | tf_op jit(solution)/shard_map/slice | solution.py:81
  25.7 9.5 %all-to-all-done = bf16[16,2,10240]{2,1,0:T(2,128)(2,1)S(1)} async-done(((bf16[16,2,10240]{2,1,0:T(2,128)(2,1)}), bf16[16,2,10240]{2,1,0:T(2,128)(2,1)S(1)}, u32[]{:S(2)}, u32[]{:S(2)}) %all-to-all-start) | async-done | bytes 655392 | tf_op jit(solution)/shard_map/all_to_all | solution.py:47
  35.2 4.0 %reshape.177 = bf16[2048,5,32]{2,1,0:T(8,128)(2,1)} reshape(bf16[16,2,10240]{2,1,0:T(2,128)(2,1)S(1)} %all-to-all-done) | data formatting | bytes 1310720
  39.2 4.5 %copy.36 = bf16[32,5,16,128]{3,1,0,2:T(8,128)(2,1)S(1)} copy(bf16[32,5,16,128]{0,1,3,2:T(8,128)(2,1)} %bitcast.98) | data formatting | bytes 1310720 | tf_op jit(solution)/shard_map/all_to_all | solution.py:47
  43.7 1.9 %fusion.70 = (bf16[528,640]{1,0:T(8,128)(2,1)}, f32[528,640]{1,0:T(8,128)}) fusion(bf16[528,512]{1,0:T(8,128)(2,1)S(1)} %bitcast.103, bf16[64,8,5,128]{3,2,1,0:T(8,128)(2,1)S(1)} %bitcast.100), kind=kOutput, calls=%fused_computation.95 | convolution fusion | flops 346368000 | bytes 3223552 | tf_op jit(solution)/shard_map/dot_general | solution.py:57
  45.6 3.1 %reshape_reshape.3 = f32[2,33,8,5,2,64]{5,4,3,2,1,0:T(2,128)S(1)} reshape(f32[528,640]{1,0:T(8,128)} %get-tuple-element.24) | data formatting | bytes 2703360 | tf_op jit(solution)/shard_map/reshape;reshape | solution.py:31
  48.7 3.5 %fusion.5 = bf16[2,33,8,5,2,64]{5,1,3,2,0,4:T(8,128)(2,1)S(1)} fusion(f32[2,33,8,5,2,64]{5,4,3,2,1,0:T(2,128)S(1)} %reshape_reshape.3, f32[2,64,64,1,1,1]{2,0,1,5,4,3:T(2,128)S(1)} %convolution_bitcast_fusion), kind=kOutput, calls=%fused_computation.4 | convolution fusion | flops 259860480 | bytes 2060288 | tf_op jit(solution)/shard_map/...ep,epq->...eq/dot_general | solution.py:32
  52.2 0.3 fusion.68
  52.5 0.7 copy.41
  53.2 0.4 squeeze.26
  53.6 0.7 copy.39
  54.3 0.4 squeeze.24
  54.8 0.3 fusion.36
  55.1 0.3 fusion.37
  55.5 0.4 fusion.71
  55.9 0.4 fusion.72
  56.2 0.4 convolution_subtract_fusion.1
  57.0 0.3 fusion.16
  57.3 0.4 fusion.15
  57.7 48.1 %all-reduce = (f32[2,33,8,16]{3,2,1,0:T(8,128)S(1)}, bf16[33,8,8]{2,1,0:T(8,128)(2,1)S(1)}, bf16[33,8,8]{2,1,0:T(8,128)(2,1)S(1)}) all-reduce(f32[2,33,8,16]{3,2,1,0:T(8,128)S(1)} %pad_maximum_fusion.1, f32[33,8,8]{2,1,0:T(8,128)S(1)} %convolution_add_fusion.1, ...), channel_id=1, replica_groups=mesh['tm'=16,'space'=2] {'tm','space'}, use_global_device_ids=true, to_apply=%region_0.1 | all-reduce | flops 12672 | bytes 92928 | tf_op jit(solution)/shard_map/psum | solution.py:77
  105.9 2.0 %fusion.33 = f32[33,16,512]{2,1,0:T(8,128)S(1)} fusion(s32[8,512]{1,0:T(8,128)S(1)} %fusion.42, f32[8,512]{1,0:T(8,128)S(1)} %get-tuple-element.21, bf16[2,33,8,16]{3,2,1,0:T(8,128)(2,1)S(1)} %get-tuple-element.17), kind=kOutput, calls=%fused_computation.50 | convolution fusion | flops 6488064 | bytes 1181696 | tf_op jit(solution)/shard_map/fbt,fbk->fkt/dot_general | solution.py:81
  107.9 2.0 %fusion.31 = f32[33,16,512]{2,1,0:T(8,128)S(1)} fusion(s32[8,512]{1,0:T(8,128)S(1)} %fusion.42, f32[8,512]{1,0:T(8,128)S(1)} %get-tuple-element.21, bf16[2,33,8,16]{3,2,1,0:T(8,128)(2,1)S(1)} %get-tuple-element.17), kind=kOutput, calls=%fused_computation.48 | convolution fusion | flops 6488064 | bytes 1181696 | tf_op jit(solution)/shard_map/fbt,fbk->fkt/dot_general | solution.py:84
  110.5 3.0 %fusion.11 = bf16[1,33,16,512]{3,2,1,0:T(8,128)(2,1)} fusion(f32[33,16,512]{2,1,0:T(8,128)S(1)} %fusion.33, f32[8,512]{1,0:T(8,128)S(1)} %get-tuple-element.22, s32[8,512]{1,0:T(8,128)S(1)} %fusion.42, bf16[2,33,8,16]{3,2,1,0:T(8,128)(2,1)S(1)} %get-tuple-element.17), kind=kOutput, calls=%fused_computation.10 | convolution fusion | flops 7028736 | bytes 1722368 | tf_op jit(solution)/shard_map/fbt,fbk->fkt/dot_general | solution.py:81
  113.5 3.0 %fusion.10 = bf16[1,33,16,512]{3,2,1,0:T(8,128)(2,1)} fusion(f32[33,16,512]{2,1,0:T(8,128)S(1)} %fusion.31, f32[8,512]{1,0:T(8,128)S(1)} %get-tuple-element.22, s32[8,512]{1,0:T(8,128)S(1)} %fusion.42, bf16[2,33,8,16]{3,2,1,0:T(8,128)(2,1)S(1)} %get-tuple-element.17), kind=kOutput, calls=%fused_computation.9 | convolution fusion | flops 7028736 | bytes 1722368 | tf_op jit(solution)/shard_map/fbt,fbk->fkt/dot_general | solution.py:84
  117.1 0.8 copy.44
  118.0 2.1 %multiply_convert_fusion = bf16[2,33,16,5,128]{4,2,3,1,0:T(8,128)(2,1)} fusion(bf16[5,128,512,1,1]{2,1,0,4,3:T(8,128)(2,1)S(1)} %bitcast.104, f32[33,16]{1,0:T(8,128)S(1)} %add_rsqrt_fusion, bf16[1,33,16,512]{3,2,1,0:T(8,128)(2,1)S(1)} %copy-done.10, bf16[1,33,16,512]{3,2,1,0:T(8,128)(2,1)S(1)} %copy-done.9), kind=kOutput, calls=%fused_computation.2 | convolution fusion | flops 695574528 | bytes 3090496 | tf_op jit(solution)/shard_map/dot_general | solution.py:92
  (39 shorter events, 2.7 us)
Async XLA Ops:
  0.6 22.2 %copy-start = (f32[8,64,64]{2,1,0:T(8,128)S(1)}, f32[8,64,64]{2,1,0:T(8,128)}, u32[]{:S(2)}) copy-start(f32[8,64,64]{2,1,0:T(8,128)} %param.7) | copy-start | bytes 393220
  6.0 12.6 %copy-start.6 = (bf16[2,33,16,5,128]{4,2,3,1,0:T(8,128)(2,1)S(1)}, bf16[2,33,16,5,128]{4,2,3,1,0:T(8,128)(2,1)}, u32[]{:S(2)}) copy-start(bf16[2,33,16,5,128]{4,2,3,1,0:T(8,128)(2,1)} %param.6) | copy-start | bytes 4055044
  11.3 24.0 %all-to-all-start = ((bf16[16,2,10240]{2,1,0:T(2,128)(2,1)}), bf16[16,2,10240]{2,1,0:T(2,128)(2,1)S(1)}, u32[]{:S(2)}, u32[]{:S(2)}) async-start(bf16[16,2,10240]{2,1,0:T(2,128)(2,1)} %reshape.176), calls=%async_computation | async-start | bytes 1310720 | tf_op jit(solution)/shard_map/all_to_all | solution.py:47
  20.8 2.0 %copy-start.8 = (s32[2]{0:T(128)S(1)}, s32[2]{0:T(128)}, u32[]{:S(2)}) copy-start(s32[2]{0:T(128)} %param.8) | copy-start | bytes 28
  21.1 2.1 %copy-start.7 = (s32[8]{0:T(128)S(1)}, s32[8]{0:T(128)}, u32[]{:S(2)}) copy-start(s32[8]{0:T(128)} %param.9) | copy-start | bytes 100
  43.6 1.9 %copy-start.1 = (bf16[32,5,16,128]{3,1,0,2:T(8,128)(2,1)}, bf16[32,5,16,128]{3,1,0,2:T(8,128)(2,1)S(1)}, u32[]{:S(2)}) copy-start(bf16[32,5,16,128]{3,1,0,2:T(8,128)(2,1)S(1)} %copy.36) | copy-start | bytes 1966084
  53.6 1.1 copy-start.5
  54.3 1.1 copy-start.4
  55.9 1.1 copy-start.3
  107.9 2.4 %copy-start.2 = (bf16[32,5,16,128]{3,1,0,2:T(8,128)(2,1)S(1)}, bf16[32,5,16,128]{3,1,0,2:T(8,128)(2,1)}, u32[]{:S(2)}) copy-start(bf16[32,5,16,128]{3,1,0,2:T(8,128)(2,1)} %copy-done.1) | copy-start | bytes 1966084
  116.5 1.5 %copy-start.9 = (bf16[1,33,16,512]{3,2,1,0:T(8,128)(2,1)S(1)}, bf16[1,33,16,512]{3,2,1,0:T(8,128)(2,1)}, u32[]{:S(2)}) copy-start(bf16[1,33,16,512]{3,2,1,0:T(8,128)(2,1)} %fusion.11) | copy-start | bytes 1622020
  116.5 1.5 %copy-start.10 = (bf16[1,33,16,512]{3,2,1,0:T(8,128)(2,1)S(1)}, bf16[1,33,16,512]{3,2,1,0:T(8,128)(2,1)}, u32[]{:S(2)}) copy-start(bf16[1,33,16,512]{3,2,1,0:T(8,128)(2,1)} %fusion.10) | copy-start | bytes 1622020
where the time goes:
time: 121 us; the launch traced here: 120 us
  blocking collectives  48.1 us (40%)
  local copies, waits for them, and re-layouts  30.1 us (25%)
  matrix products  21.4 us (18%)
  waiting for transfers between devices  9.49 us (8%)
  starting transfers between devices  7.39 us (6%)
  other arithmetic  2.59 us (2%)
    psum x1, blocking collectives, on_device(): lax.psum((coeff_part, gram_real, gram_imag), ('tm', 'space'))  48.1 us
    unnamed x27, local copies, waits for them, and re-layouts  15.7 us
    all_to_all x1, waiting for transfers between devices, on_device(): lax.all_to_all(snapshots, 'tm', split_axis=2, concat_axis=0, tiled=True)  9.49 us
    all_to_all x1, starting transfers between devices, on_device(): lax.all_to_all(snapshots, 'tm', split_axis=2, concat_axis=0, tiled=True)  7.39 us
    all_to_all x1, local copies, waits for them, and re-layouts, on_device(): lax.all_to_all(snapshots, 'tm', split_axis=2, concat_axis=0, tiled=True)  4.46 us
    dot_general x1, matrix products, apply_mass(): jnp.einsum('...ep,epq->...eq', shaped, local_mass, precision=lax.Precisio...  3.49 us
    another operation x1, local copies, waits for them, and re-layouts, apply_mass(): shaped = field.reshape(lead + (elem_count, local_mass.shape[1]))  3.11 us
    dot_general x1, matrix products, on_device(): jnp.einsum('fbt,fbk->fkt', table_float[1], coeff_round[1])  3.02 us
  transfers between devices with their start and end apart: 1, of which 1 were waited for; matrix products, arithmetic and copies ran while one was open for 6% of the time, Pallas kernels for 0%

commit v1 on v0

v1 whole, which is shorter than its diff:
```python
import functools
import math

import jax
import jax.numpy as jnp
from jax import lax
from jax.experimental import pallas as pl
from jax.experimental.pallas import tpu as pltpu
from jax.sharding import PartitionSpec as P

NT = 256
GROUP = 8
MESH = pl.DeviceIdType.MESH
BF = jnp.bfloat16
F32 = jnp.float32


def mm(a, b, contract):
    return lax.dot_general(a, b, (contract, ((), ())), preferred_element_type=F32)


def kernel(
    n_tm, n_sp, entries,
    snap, basis, mass, kinds, offs,
    coef_out, new_out,
    table, rec, ub, sh, wt, xb, slots, yb, ob,
    a_send, a_recv, b_sem, s1, r1, s2, r2, o_sem,
):
    n = n_tm * n_sp
    tm = lax.axis_index("tm")
    sp = lax.axis_index("space")
    me = sp * n_tm + tm
    freqs = basis.shape[1]
    nvar, rows, pts = rec.shape[1:]
    groups = sh.shape[0] // (2 * GROUP * 8)
    record = n_tm * rows
    blocks = offs.shape[0]
    modes = basis.shape[3]
    upo = slots.shape[1]
    owners = xb.shape[0] // upo
    half = GROUP * blocks
    lanes = GROUP * modes

    def device(d):
        return {"tm": lax.rem(d, n_tm), "space": lax.div(d, n_tm)}

    barrier = pltpu.get_barrier_semaphore()

    def greet(i, carry):
        pl.semaphore_signal(barrier, inc=1, device_id=device(lax.rem(me + i, n)), device_id_type=MESH)
        return carry

    lax.fori_loop(1, n, greet, 0)
    load_basis = pltpu.make_async_copy(basis, ub.at[:, pl.ds(0, freqs)], b_sem)
    load_basis.start()
    pl.semaphore_wait(barrier, n - 1)

    def send(i, carry):
        to = lax.rem(tm + i, n_tm)
        pltpu.make_async_remote_copy(
            snap.at[:, :, pl.ds(pl.multiple_of(to * pts, pts), pts)],
            rec.at[tm], a_send, a_recv, device_id={"tm": to, "space": sp}, device_id_type=MESH,
        ).start()
        return carry

    lax.fori_loop(1, n_tm, send, 0)
    pltpu.make_async_copy(
        snap.at[:, :, pl.ds(pl.multiple_of(tm * pts, pts), pts)], rec.at[tm], a_recv
    ).start()

    row = lax.broadcasted_iota(jnp.int32, (blocks, record), 0)
    lag = lax.broadcasted_iota(jnp.int32, (blocks, record), 1)
    for b in range(blocks):
        lag = jnp.where(row == b, lag - offs[b], lag)
    inside = (lag >= 0) & (lag < NT)
    theta = jnp.clip(lag, 0, NT - 1).astype(F32) * (2.0 * math.pi / NT)
    c1, s1v = jnp.cos(theta), jnp.sin(theta)
    win = jnp.where(inside, (0.5 - 0.5 * c1) * (1.0 / math.sqrt(0.375 * NT)), 0.0)
    cc, ss = win, jnp.zeros_like(win)
    for f in range(0, groups * GROUP, 2):
        c_next, s_next = cc * c1 - ss * s1v, ss * c1 + cc * s1v
        at = (f // GROUP) * 2 * half + (f % GROUP) * blocks
        table[at : at + 2 * blocks] = jnp.concatenate([cc, c_next], axis=0).astype(BF)
        table[at + half : at + half + 2 * blocks] = jnp.concatenate([-ss, -s_next], axis=0).astype(BF)
        cc, ss = c_next * c1 - s_next * s1v, s_next * c1 + c_next * s1v

    size = mass.shape[1]
    elems = pts // size
    strips = []
    for e in range(elems):
        kind = jnp.full((size, size), kinds[e], jnp.int32)
        blk = mass[0]
        for k in range(1, mass.shape[0]):
            blk = jnp.where(kind == k, mass[k], blk)
        zero = jnp.zeros_like(blk)
        strips.append(jnp.concatenate([blk if j == e else zero for j in range(elems)], axis=1))
    m_all = jnp.concatenate(strips, axis=0)
    m_hi = m_all.astype(BF)
    m_lo = (m_all - m_hi.astype(F32)).astype(BF)
    m_stack = jnp.concatenate([m_hi, m_hi, m_lo], axis=0)

    load_basis.wait()
    ub[:, freqs:] = jnp.zeros((2, groups * GROUP - freqs) + ub.shape[2:], BF)

    pltpu.make_async_copy(rec, rec, a_recv).wait()
    x = jnp.concatenate([rec[:, v].reshape(record, pts) for v in range(nvar)], axis=1)
    spec = mm(table[...], x, ((1,), (0,)))
    s_hi = spec.astype(BF)
    s_lo = (spec - s_hi.astype(F32)).astype(BF)
    sh[...] = s_hi
    for v in range(nvar):
        cut = slice(v * pts, (v + 1) * pts)
        lhs = jnp.concatenate([s_hi[:, cut], s_lo[:, cut], s_hi[:, cut]], axis=1)
        wt[:, cut] = mm(lhs, m_stack, ((1,), (0,))).astype(BF)

    row_f = lax.broadcasted_iota(jnp.int32, (GROUP, blocks, lanes), 0)
    lane = lax.broadcasted_iota(jnp.int32, (GROUP, blocks, lanes), 2)
    diag_k = row_f == lane // modes
    diag_b = row_f == (lane % half) // blocks
    lane2 = lax.broadcasted_iota(jnp.int32, (blocks, lanes), 1)

    def fold(full, mask):
        return jnp.sum(jnp.where(mask, full.reshape(GROUP, blocks, lanes), 0.0), axis=0)

    def put(i, val):
        h = blocks // 2
        xb[2 * i] = val[:h]
        xb[2 * i + 1] = val[h:]

    def get(i):
        return jnp.concatenate([yb[2 * i], yb[2 * i + 1]], axis=0)

    for g in range(groups):
        top = g * 2 * half
        w_g = wt[top : top + 2 * half]
        f0 = g * GROUP
        u = [
            jnp.concatenate(
                [ub[c, f0 : f0 + GROUP, v].reshape(lanes, pts) for v in range(nvar)], axis=1
            )
            for c in range(2)
        ]
        lhs = jnp.concatenate(u + [sh[top : top + 2 * half]], axis=0)
        full = mm(w_g, lhs, ((1,), (1,)))
        rr = fold(full[:half, :lanes], diag_k)
        ri = fold(full[:half, lanes : 2 * lanes], diag_k)
        ir = fold(full[half:, :lanes], diag_k)
        ii = fold(full[half:, lanes : 2 * lanes], diag_k)
        p_r = fold(full[:half, 2 * lanes :], diag_b)
        p_i = pltpu.roll(fold(full[half:, 2 * lanes :], diag_b), half, 1)
        put(3 * g, rr + ii)
        put(3 * g + 1, ir - ri)
        put(3 * g + 2, jnp.where(lane2 < half, p_r + p_i, p_i - p_r))

    def scatter(i, carry):
        o = lax.rem(me + i, owners)

        @pl.when(o != me)
        def _():
            pltpu.make_async_remote_copy(
                xb.at[pl.ds(o * upo, upo)], slots.at[me], s1, r1,
                device_id=device(o), device_id_type=MESH,
            ).start()

        return carry

    lax.fori_loop(0, owners, scatter, 0)

    @pl.when(me < owners)
    def _():
        pltpu.make_async_copy(xb.at[pl.ds(me * upo, upo)], slots.at[me], r1).start()
        pltpu.make_async_copy(slots, slots, r1).wait()
        yb[pl.ds(me * upo, upo)] = jnp.sum(slots[...], axis=0)

        def spread(i, carry):
            pltpu.make_async_remote_copy(
                yb.at[pl.ds(me * upo, upo)], yb.at[pl.ds(me * upo, upo)], s2, r2,
                device_id=device(lax.rem(me + i, n)), device_id_type=MESH,
            ).start()
            return carry

        lax.fori_loop(1, n, spread, 0)
        part = yb.at[pl.ds(0, (owners - 1) * upo)]
        pltpu.make_async_copy(part, part, r2).wait()

    @pl.when(me >= owners)
    def _():
        pltpu.make_async_copy(yb, yb, r2).wait()

    scale = 1.0 / math.sqrt(entries)
    outs = []
    for g in range(groups):
        top = g * 2 * half
        f0 = g * GROUP
        nf = min(GROUP, freqs - f0)
        co_r, co_i = get(3 * g) * scale, get(3 * g + 1) * scale
        coef_out[0, g] = co_r
        coef_out[1, g] = co_i
        cr = co_r.astype(BF).astype(F32)
        ci = co_i.astype(BF).astype(F32)
        gram = get(3 * g + 2)

        def spread_rows(val, mask):
            big = jnp.broadcast_to(val[None], (GROUP, blocks, lanes))
            return jnp.where(mask, big, 0.0).reshape(half, lanes)

        d_r, d_i = spread_rows(cr, diag_k), spread_rows(ci, diag_k)
        turned = pltpu.roll(gram, half, 1)
        turned = jnp.where(lane2 < half, -turned, turned)
        quad = jnp.concatenate([spread_rows(gram, diag_b), spread_rows(turned, diag_b)], axis=0)
        vec = jnp.concatenate([d_r, d_i], axis=0)
        energy = jnp.sum(vec * mm(quad.astype(BF), vec.astype(BF), ((1,), (0,))), axis=0, keepdims=True)
        factor = 1.0 / jnp.sqrt(energy / entries + 1e-06)
        fac = jnp.transpose(jnp.broadcast_to(factor, (pts, lanes)))
        s_g = sh[top : top + 2 * half]
        for c in range(2):
            d = jnp.concatenate([d_r, -d_i] if c == 0 else [d_i, d_r], axis=0)
            field = mm(jnp.transpose(d).astype(BF), s_g, ((1,), (0,)))
            for v in range(nvar):
                val = (field[:, v * pts : (v + 1) * pts] * fac).astype(BF).reshape(GROUP, modes, pts)
                ob[c, f0 : f0 + nf, v] = val[:nf]
        cp = pltpu.make_async_copy(ob.at[:, pl.ds(f0, nf)], new_out.at[:, pl.ds(f0, nf)], o_sem.at[g])
        cp.start()
        outs.append(cp)

    for cp in outs:
        cp.wait()
    first = rec.at[pl.ds(0, n_tm - 1)]
    pltpu.make_async_copy(first, first, a_send).wait()

    @pl.when(me < owners)
    def _():
        part = xb.at[pl.ds(0, (owners - 1) * upo)]
        pltpu.make_async_copy(part, part, s1).wait()
        whole = slots.at[pl.ds(0, n - 1)]
        pltpu.make_async_copy(whole, whole, s2).wait()

    @pl.when(me >= owners)
    def _():
        pltpu.make_async_copy(xb, xb, s1).wait()


def solution(mesh):
    n_tm, n_sp = mesh.shape["tm"], mesh.shape["space"]
    n = n_tm * n_sp

    def on_device(snapshots, basis, mass_table, elem_kind, offsets):
        rows, nvar, slab = snapshots.shape
        _, freqs, modes, _, pts = basis.shape
        blocks = offsets.shape[0]
        groups = -(-freqs // GROUP)
        entries = nvar * pts * n
        units = 6 * groups
        upo = -(-units // n)
        owners = -(-units // upo)
        table_rows = groups * 2 * GROUP * blocks
        unit = (blocks // 2, GROUP * modes)
        snap = jnp.transpose(snapshots, (1, 0, 2))
        base = jnp.transpose(basis, (0, 1, 3, 2, 4))
        any_spec = pl.BlockSpec(memory_space=pl.ANY)
        vmem = pl.BlockSpec(memory_space=pltpu.VMEM)
        smem = pl.BlockSpec(memory_space=pltpu.SMEM)
        coef, new = pl.pallas_call(
            functools.partial(kernel, n_tm, n_sp, entries),
            out_shape=(
                jax.ShapeDtypeStruct((2, groups, blocks, GROUP * modes), F32),
                jax.ShapeDtypeStruct(base.shape, BF),
            ),
            in_specs=[any_spec, any_spec, vmem, smem, smem],
            out_specs=(vmem, any_spec),
            scratch_shapes=[
                pltpu.VMEM((table_rows, rows * n_tm), BF),
                pltpu.VMEM((n_tm, nvar, rows, pts), BF),
                pltpu.VMEM((2, groups * GROUP, nvar, modes, pts), BF),
                pltpu.VMEM((table_rows, nvar * pts), BF),
                pltpu.VMEM((table_rows, nvar * pts), BF),
                pltpu.VMEM((owners * upo,) + unit, F32),
                pltpu.VMEM((n, upo) + unit, F32),
                pltpu.VMEM((owners * upo,) + unit, F32),
                pltpu.VMEM((2, freqs, nvar, modes, pts), BF),
            ]
            + [pltpu.SemaphoreType.DMA] * 7
            + [pltpu.SemaphoreType.DMA((groups,))],
            compiler_params=pltpu.CompilerParams(
                collective_id=0, has_side_effects=True, vmem_limit_bytes=48 * 1024 * 1024
            ),
        )(snap, base, mass_table, elem_kind, offsets)
        coef = coef.reshape(2, groups, blocks, GROUP, modes).transpose(0, 1, 3, 2, 4)
        coef = coef.reshape(2, groups * GROUP, blocks, modes)[:, :freqs]
        return coef, jnp.transpose(new, (0, 1, 3, 2, 4))

    return jax.shard_map(
        on_device,
        mesh=mesh,
        in_specs=(
            P("tm", None, "space"),
            P(None, None, None, None, ("space", "tm")),
            P(),
            P(("space", "tm")),
            P(),
        ),
        out_specs=(P(), P(None, None, None, None, ("space", "tm"))),
        check_vma=False,
    )
```

time: 121 us -> 43.4 us (0.36)
  blocking collectives: 48.1 us -> 0 us
  Pallas kernels: 0 us -> 35.6 us
  local copies, waits for them, and re-layouts: 30.1 us -> 6.8 us
  matrix products: 21.4 us -> 0 us
  waiting for transfers between devices: 9.49 us -> 0 us
  starting transfers between devices: 7.39 us -> 0 us
  other arithmetic: 2.59 us -> 0 us
    psum x1 -> x0, blocking collectives: 48.1 us -> none  [on_device(): lax.psum((coeff_part, gram_real, gram_imag), ('tm', 'space'))]
    pallas_call x0 -> x1, Pallas kernels: none -> 35.6 us  [on_device(): pl.pallas_call(functools.partial(kernel, n_tm, n_sp, entries), out_shape=...]
    dot_general x20 -> x0, matrix products: 21.4 us -> none  [the longest x1 3.49 us: apply_mass(): jnp.einsum('...ep,epq->...eq', shaped, local_mass, precision=lax.Precisio...]
    all_to_all x1 -> x0, waiting for transfers between devices: 9.49 us -> none  [on_device(): lax.all_to_all(snapshots, 'tm', split_axis=2, concat_axis=0, tiled=True)]
    unnamed x27 -> x12, local copies, waits for them, and re-layouts: 15.7 us -> 6.58 us
    all_to_all x1 -> x0, starting transfers between devices: 7.39 us -> none  [on_device(): lax.all_to_all(snapshots, 'tm', split_axis=2, concat_axis=0, tiled=True)]
    all_to_all x1 -> x0, local copies, waits for them, and re-layouts: 4.46 us -> none  [on_device(): lax.all_to_all(snapshots, 'tm', split_axis=2, concat_axis=0, tiled=True)]
    squeeze x4 -> x0, local copies, waits for them, and re-layouts: 4.09 us -> none  [the longest x1 1.65 us: paired_einsum(): first_pair[1]]
  transfers between devices with their start and end apart: 1 -> 0, of which waited for: 1 -> 0; matrix products, arithmetic and copies ran while one was open for 6% -> 0% of each run, Pallas kernels for 0% -> 0%
where the time goes in v1:
time: 43.4 us; the launch traced here: 43.1 us
  Pallas kernels  35.6 us (82%)
  local copies, waits for them, and re-layouts  6.8 us (16%)
  between operations  0.68 us (2%)
    pallas_call x1, Pallas kernels, on_device(): pl.pallas_call(functools.partial(kernel, n_tm, n_sp, entries), out_shape=...  35.6 us
    unnamed x12, local copies, waits for them, and re-layouts  6.58 us

profile of v1, /device:TPU:0, one launch (start us, length us, event | category | flops | bytes accessed | tf_op | source)
XLA Modules:
  0.0 43.1 jit_solution(13385313826201630523)
XLA Ops:
  0.6 0.0 copy-start
  0.6 1.3 %copy-done = bf16[2,33,16,5,128]{4,2,3,1,0:T(8,128)(2,1)S(1)} copy-done((bf16[2,33,16,5,128]{4,2,3,1,0:T(8,128)(2,1)S(1)}, bf16[2,33,16,5,128]{4,2,3,1,0:T(8,128)(2,1)}, u32[]{:S(2)}) %copy-start) | copy-done | bytes 1351704
  2.0 0.0 copy-start.1
  2.0 1.1 %copy-done.1 = bf16[32,5,2048]{2,0,1:T(8,128)(2,1)S(1)} copy-done((bf16[32,5,2048]{2,0,1:T(8,128)(2,1)S(1)}, bf16[32,5,2048]{2,0,1:T(8,128)(2,1)}, u32[]{:S(2)}) %copy-start.1) | copy-done | bytes 655384
  3.1 0.0 copy-start.2
  3.1 0.9 %copy-done.2 = f32[8,64,64]{2,1,0:T(8,128)S(1)} copy-done((f32[8,64,64]{2,1,0:T(8,128)S(1)}, f32[8,64,64]{2,1,0:T(8,128)}, u32[]{:S(2)}) %copy-start.2) | copy-done | bytes 131096
  4.0 0.0 copy-start.3
  4.0 0.7 %copy-done.3 = s32[2]{0:T(128)S(1)} copy-done((s32[2]{0:T(128)S(1)}, s32[2]{0:T(128)}, u32[]{:S(2)}) %copy-start.3) | copy-done | bytes 32
  4.7 0.0 copy-start.4
  4.7 0.7 %copy-done.4 = s32[8]{0:T(128)S(1)} copy-done((s32[8]{0:T(128)S(1)}, s32[8]{0:T(128)}, u32[]{:S(2)}) %copy-start.4) | copy-done | bytes 56
  5.3 35.6 %shard_map.68 = (f32[2,5,8,128]{3,2,1,0:T(8,128)S(1)}, bf16[2,33,5,16,128]{4,3,2,1,0:T(8,128)(2,1)S(1)}) custom-call(bf16[5,32,2048]{2,1,0:T(8,128)(2,1)S(1)} %bitcast.10, bf16[2,33,5,16,128]{4,3,2,1,0:T(8,128)(2,1)S(1)} %bitcast.8, f32[8,64,64]{2,1,0:T(8,128)S(1)} %copy-done.2, s32[2]{0:T(128)S(1)} %copy-done.3, s32[8]{0:T(128)S(1)} %copy-done.4), custom_call_target="tpu_custom_call" | custom-call | tf_op jit(solution)/shard_map/pallas_call | solution.py:263
  41.0 0.1 reshape.10
  41.1 0.1 copy.8
  41.2 0.8 %copy.9 = f32[2,33,8,16]{1,3,2,0:T(8,128)} copy(f32[2,33,8,16]{3,2,1,0:T(8,128)S(1)} %slice.4) | data formatting | bytes 67584
  42.1 1.1 %copy.11 = bf16[2,33,16,5,128]{4,2,3,1,0:T(8,128)(2,1)} copy(bf16[2,33,16,5,128]{4,2,3,1,0:T(8,128)(2,1)S(1)} %bitcast.9) | data formatting | bytes 2703360
  (1 shorter events, 0.0 us)
Async XLA Ops:
  0.6 1.3 %copy-start = (bf16[2,33,16,5,128]{4,2,3,1,0:T(8,128)(2,1)S(1)}, bf16[2,33,16,5,128]{4,2,3,1,0:T(8,128)(2,1)}, u32[]{:S(2)}) copy-start(bf16[2,33,16,5,128]{4,2,3,1,0:T(8,128)(2,1)} %param.6) | copy-start | bytes 4055044
  2.0 1.1 %copy-start.1 = (bf16[32,5,2048]{2,0,1:T(8,128)(2,1)S(1)}, bf16[32,5,2048]{2,0,1:T(8,128)(2,1)}, u32[]{:S(2)}) copy-start(bf16[32,5,2048]{2,0,1:T(8,128)(2,1)} %param.5) | copy-start | bytes 1966084
  3.1 0.9 %copy-start.2 = (f32[8,64,64]{2,1,0:T(8,128)S(1)}, f32[8,64,64]{2,1,0:T(8,128)}, u32[]{:S(2)}) copy-start(f32[8,64,64]{2,1,0:T(8,128)} %mass.1) | copy-start | bytes 393220
  4.0 0.7 %copy-start.3 = (s32[2]{0:T(128)S(1)}, s32[2]{0:T(128)}, u32[]{:S(2)}) copy-start(s32[2]{0:T(128)} %kinds.1) | copy-start | bytes 28
  4.7 0.7 %copy-start.4 = (s32[8]{0:T(128)S(1)}, s32[8]{0:T(128)}, u32[]{:S(2)}) copy-start(s32[8]{0:T(128)} %offs.1) | copy-start | bytes 100

commit v2 on v1

v2 whole, which is shorter than its diff:
```python
import functools
import math

import jax
import jax.numpy as jnp
from jax import lax
from jax.experimental import pallas as pl
from jax.experimental.pallas import tpu as pltpu
from jax.sharding import PartitionSpec as P

NT = 256
GROUP = 8
MESH = pl.DeviceIdType.MESH
BF = jnp.bfloat16
F32 = jnp.float32


def mm(a, b, contract):
    return lax.dot_general(a, b, (contract, ((), ())), preferred_element_type=F32)


def kernel(
    n_tm, n_sp, low, entries, chunks,
    snap, basis, mass_in, kinds_in, offs_in,
    coef_out, new_out,
    table, ub, sh, xb, line, plane, yb, mass, kinds, offs, *rest,
):
    recs, (a_send, a_recv, l_sem, s1, r1, s2, r2, s3, r3) = rest[: len(chunks)], rest[len(chunks) :]
    tm = lax.axis_index("tm")
    sp = lax.axis_index("space")
    high = n_tm // low
    side = low * n_sp
    spot = sp * low + lax.rem(tm, low)
    level = lax.div(tm, low)
    freqs = basis.shape[1]
    rows, pts = recs[0].shape[2:]
    groups = sh.shape[0] // (2 * GROUP * 8)
    record = n_tm * rows
    blocks = offs.shape[0]
    modes = basis.shape[3]
    upo = plane.shape[1]
    owners = xb.shape[0] // upo
    half = GROUP * blocks
    lanes = GROUP * modes

    def beside(p):
        return {"tm": level * low + lax.rem(p, low), "space": lax.div(p, low)}

    barrier = pltpu.get_barrier_semaphore()

    def greet_line(i, carry):
        pl.semaphore_signal(
            barrier, inc=1, device_id={"tm": lax.rem(tm + i, n_tm), "space": sp}, device_id_type=MESH
        )
        return carry

    def greet_side(i, carry):
        to = lax.rem(sp + lax.div(i, low), n_sp)
        pl.semaphore_signal(
            barrier, inc=1, device_id={"tm": level * low + lax.rem(i, low), "space": to}, device_id_type=MESH
        )
        return carry

    lax.fori_loop(1, n_tm, greet_line, 0)
    lax.fori_loop(low, side, greet_side, 0)
    loads = [
        pltpu.make_async_copy(offs_in, offs, l_sem.at[0]),
        pltpu.make_async_copy(kinds_in, kinds, l_sem.at[1]),
        pltpu.make_async_copy(mass_in, mass, l_sem.at[2]),
        pltpu.make_async_copy(basis, ub.at[:, pl.ds(0, freqs)], l_sem.at[3]),
    ]
    for cp in loads:
        cp.start()
    pl.semaphore_wait(barrier, n_tm - 1 + side - low)

    for ci, (v0, v1) in enumerate(chunks):

        def block(to):
            return snap.at[pl.ds(v0, v1 - v0), :, pl.ds(pl.multiple_of(to * pts, pts), pts)]

        def send(i, carry):
            d = lax.div(i + 1, 2)
            to = lax.rem(tm + n_tm // 2 + jnp.where(lax.rem(i, 2) == 0, d, -d) + n_tm, n_tm)
            pltpu.make_async_remote_copy(
                block(to), recs[ci].at[tm], a_send.at[ci], a_recv.at[ci],
                device_id={"tm": to, "space": sp}, device_id_type=MESH,
            ).start()
            return carry

        lax.fori_loop(0, n_tm - 1, send, 0)
        pltpu.make_async_copy(block(tm), recs[ci].at[tm], a_recv.at[ci]).start()

    loads[0].wait()
    row = lax.broadcasted_iota(jnp.int32, (blocks, record), 0)
    lag = lax.broadcasted_iota(jnp.int32, (blocks, record), 1)
    for b in range(blocks):
        lag = jnp.where(row == b, lag - offs[b], lag)
    inside = (lag >= 0) & (lag < NT)
    theta = jnp.clip(lag, 0, NT - 1).astype(F32) * (2.0 * math.pi / NT)
    c1, s1v = jnp.cos(theta), jnp.sin(theta)
    win = jnp.where(inside, (0.5 - 0.5 * c1) * (1.0 / math.sqrt(0.375 * NT)), 0.0)
    cc, ss = win, jnp.zeros_like(win)
    for f in range(0, groups * GROUP, 2):
        c_next, s_next = cc * c1 - ss * s1v, ss * c1 + cc * s1v
        at = (f // GROUP) * 2 * half + (f % GROUP) * blocks
        table[at : at + 2 * blocks] = jnp.concatenate([cc, c_next], axis=0).astype(BF)
        table[at + half : at + half + 2 * blocks] = jnp.concatenate([-ss, -s_next], axis=0).astype(BF)
        cc, ss = c_next * c1 - s_next * s1v, s_next * c1 + c_next * s1v

    loads[1].wait()
    loads[2].wait()
    size = mass.shape[1]
    elems = pts // size
    strips = []
    for e in range(elems):
        kind = jnp.full((size, size), kinds[e], jnp.int32)
        blk = mass[0]
        for k in range(1, mass.shape[0]):
            blk = jnp.where(kind == k, mass[k], blk)
        zero = jnp.zeros_like(blk)
        strips.append(jnp.concatenate([blk if j == e else zero for j in range(elems)], axis=1))
    m_all = jnp.concatenate(strips, axis=0)
    m_hi = m_all.astype(BF)
    m_lo = (m_all - m_hi.astype(F32)).astype(BF)
    m_stack = jnp.concatenate([m_hi, m_hi, m_lo], axis=0)

    loads[3].wait()
    ub[:, freqs:] = jnp.zeros((2, groups * GROUP - freqs) + ub.shape[2:], BF)

    row_f = lax.broadcasted_iota(jnp.int32, (GROUP, blocks, lanes), 0)
    lane = lax.broadcasted_iota(jnp.int32, (GROUP, blocks, lanes), 2)
    diag_k = row_f == lane // modes
    diag_b = row_f == (lane % half) // blocks
    lane2 = lax.broadcasted_iota(jnp.int32, (blocks, lanes), 1)

    def fold(full, mask):
        return jnp.sum(jnp.where(mask, full.reshape(GROUP, blocks, lanes), 0.0), axis=0)

    total = [None] * (3 * groups)
    for ci, (v0, v1) in enumerate(chunks):
        rec = recs[ci]
        pltpu.make_async_copy(rec, rec, a_recv.at[ci]).wait()
        count = v1 - v0
        x = jnp.concatenate([rec[:, v].reshape(record, pts) for v in range(count)], axis=1)
        spec = mm(table[...], x, ((1,), (0,)))
        s_hi = spec.astype(BF)
        s_lo = (spec - s_hi.astype(F32)).astype(BF)
        sh[:, v0 * pts : v1 * pts] = s_hi
        wts = []
        for v in range(count):
            cut = slice(v * pts, (v + 1) * pts)
            lhs = jnp.concatenate([s_hi[:, cut], s_lo[:, cut], s_hi[:, cut]], axis=1)
            wts.append(mm(lhs, m_stack, ((1,), (0,))).astype(BF))
        wt = jnp.concatenate(wts, axis=1)
        for g in range(groups):
            top = g * 2 * half
            f0 = g * GROUP
            u = [
                jnp.concatenate(
                    [ub[c, f0 : f0 + GROUP, v].reshape(lanes, pts) for v in range(v0, v1)], axis=1
                )
                for c in range(2)
            ]
            lhs = jnp.concatenate(u + [s_hi[top : top + 2 * half]], axis=0)
            full = mm(wt[top : top + 2 * half], lhs, ((1,), (1,)))
            rr = fold(full[:half, :lanes], diag_k)
            ri = fold(full[:half, lanes : 2 * lanes], diag_k)
            ir = fold(full[half:, :lanes], diag_k)
            ii = fold(full[half:, lanes : 2 * lanes], diag_k)
            p_r = fold(full[:half, 2 * lanes :], diag_b)
            p_i = pltpu.roll(fold(full[half:, 2 * lanes :], diag_b), half, 1)
            new = [rr + ii, ir - ri, jnp.where(lane2 < half, p_r + p_i, p_i - p_r)]
            for j in range(3):
                at = 3 * g + j
                total[at] = new[j] if ci == 0 else total[at] + new[j]
    for at in range(3 * groups):
        xb[at] = total[at]

    mine = pl.ds(spot * upo, upo)

    def scatter(i, carry):
        o = lax.rem(spot + i, owners)

        @pl.when(o != spot)
        def _():
            pltpu.make_async_remote_copy(
                xb.at[pl.ds(o * upo, upo)], plane.at[spot], s1, r1,
                device_id=beside(o), device_id_type=MESH,
            ).start()

        return carry

    lax.fori_loop(0, owners, scatter, 0)

    def wait_bytes(ref, sem):
        pltpu.make_async_copy(ref, ref, sem).wait()

    @pl.when(spot < owners)
    def _():
        plane[spot] = xb[mine]
        wait_bytes(plane.at[pl.ds(0, side - 1)], r1)
        line[level] = jnp.sum(plane[...], axis=0)

        def exchange(i, carry):
            to = lax.rem(level + i, high) * low + lax.rem(tm, low)
            pltpu.make_async_remote_copy(
                line.at[level], line.at[level], s2, r2,
                device_id={"tm": to, "space": sp}, device_id_type=MESH,
            ).start()
            return carry

        if high > 1:
            lax.fori_loop(1, high, exchange, 0)
            wait_bytes(line.at[pl.ds(0, high - 1)], r2)
        yb[mine] = jnp.sum(line[...], axis=0)

        def gather(i, carry):
            pltpu.make_async_remote_copy(
                yb.at[mine], yb.at[mine], s3, r3,
                device_id=beside(lax.rem(spot + i, side)), device_id_type=MESH,
            ).start()
            return carry

        lax.fori_loop(1, side, gather, 0)
        wait_bytes(yb.at[pl.ds(0, (owners - 1) * upo)], r3)

    @pl.when(spot >= owners)
    def _():
        wait_bytes(yb, r3)

    scale = 1.0 / math.sqrt(entries)
    nvar = sh.shape[1] // pts
    for g in range(groups):
        top = g * 2 * half
        f0 = g * GROUP
        nf = min(GROUP, freqs - f0)
        co_r, co_i = yb[3 * g] * scale, yb[3 * g + 1] * scale
        coef_out[0, g] = co_r
        coef_out[1, g] = co_i
        cr = co_r.astype(BF).astype(F32)
        ci = co_i.astype(BF).astype(F32)
        gram = yb[3 * g + 2]

        def spread_rows(val, mask):
            big = jnp.broadcast_to(val[None], (GROUP, blocks, lanes))
            return jnp.where(mask, big, 0.0).reshape(half, lanes)

        d_r, d_i = spread_rows(cr, diag_k), spread_rows(ci, diag_k)
        turned = pltpu.roll(gram, half, 1)
        turned = jnp.where(lane2 < half, -turned, turned)
        quad = jnp.concatenate([spread_rows(gram, diag_b), spread_rows(turned, diag_b)], axis=0)
        vec = jnp.concatenate([d_r, d_i], axis=0)
        energy = jnp.sum(vec * mm(quad.astype(BF), vec.astype(BF), ((1,), (0,))), axis=0, keepdims=True)
        factor = 1.0 / jnp.sqrt(energy / entries + 1e-06)
        fac = jnp.transpose(jnp.broadcast_to(factor, (pts, lanes)))
        s_g = sh[top : top + 2 * half]
        for c in range(2):
            d = jnp.concatenate([d_r, -d_i] if c == 0 else [d_i, d_r], axis=0)
            field = mm(jnp.transpose(d).astype(BF), s_g, ((1,), (0,)))
            for v in range(nvar):
                val = (field[:, v * pts : (v + 1) * pts] * fac).astype(BF).reshape(GROUP, modes, pts)
                new_out[c, f0 : f0 + nf, v] = val[:nf]

    for ci in range(len(chunks)):
        wait_bytes(recs[ci].at[pl.ds(0, n_tm - 1)], a_send.at[ci])

    @pl.when(spot < owners)
    def _():
        wait_bytes(xb.at[pl.ds(0, (owners - 1) * upo)], s1)
        if high > 1:
            wait_bytes(line.at[pl.ds(0, high - 1)], s2)
        wait_bytes(plane.at[pl.ds(0, side - 1)], s3)

    @pl.when(spot >= owners)
    def _():
        wait_bytes(xb, s1)


def solution(mesh):
    n_tm, n_sp = mesh.shape["tm"], mesh.shape["space"]
    n = n_tm * n_sp

    def on_device(snapshots, basis, mass_table, elem_kind, offsets):
        rows, nvar, slab = snapshots.shape
        _, freqs, modes, _, pts = basis.shape
        blocks = offsets.shape[0]
        groups = -(-freqs // GROUP)
        entries = nvar * pts * n
        units = 3 * groups
        low = math.gcd(n_tm, 4)
        side = low * n_sp
        upo = -(-units // side)
        owners = -(-units // upo)
        table_rows = groups * 2 * GROUP * blocks
        unit = (blocks, GROUP * modes)
        chunks = tuple((v, min(v + 2, nvar)) for v in range(0, nvar, 2))
        snap = jnp.transpose(snapshots, (1, 0, 2))
        base = jnp.transpose(basis, (0, 1, 3, 2, 4))
        hbm = pl.BlockSpec(memory_space=pltpu.HBM)
        vmem = pl.BlockSpec(memory_space=pltpu.VMEM)
        coef, new = pl.pallas_call(
            functools.partial(kernel, n_tm, n_sp, low, entries, chunks),
            out_shape=(
                jax.ShapeDtypeStruct((2, groups, blocks, GROUP * modes), F32),
                jax.ShapeDtypeStruct(base.shape, BF),
            ),
            in_specs=[hbm] * 5,
            out_specs=(vmem, vmem),
            scratch_shapes=[
                pltpu.VMEM((table_rows, rows * n_tm), BF),
                pltpu.VMEM((2, groups * GROUP, nvar, modes, pts), BF),
                pltpu.VMEM((table_rows, nvar * pts), BF),
                pltpu.VMEM((owners * upo,) + unit, F32),
                pltpu.VMEM((n_tm // low, upo) + unit, F32),
                pltpu.VMEM((side, upo) + unit, F32),
                pltpu.VMEM((owners * upo,) + unit, F32),
                pltpu.VMEM(mass_table.shape, F32),
                pltpu.SMEM(elem_kind.shape, jnp.int32),
                pltpu.SMEM(offsets.shape, jnp.int32),
            ]
            + [pltpu.VMEM((n_tm, v1 - v0, rows, pts), BF) for v0, v1 in chunks]
            + [
                pltpu.SemaphoreType.DMA((len(chunks),)),
                pltpu.SemaphoreType.DMA((len(chunks),)),
                pltpu.SemaphoreType.DMA((4,)),
            ]
            + [pltpu.SemaphoreType.DMA] * 6,
            compiler_params=pltpu.CompilerParams(
                collective_id=0, has_side_effects=True, vmem_limit_bytes=48 * 1024 * 1024
            ),
        )(*[pltpu.with_memory_space_constraint(a, pltpu.HBM) for a in (snap, base, mass_table, elem_kind, offsets)])
        coef = coef.reshape(2, groups, blocks, GROUP, modes).transpose(0, 1, 3, 2, 4)
        coef = coef.reshape(2, groups * GROUP, blocks, modes)[:, :freqs]
        return coef, jnp.transpose(new, (0, 1, 3, 2, 4))

    return jax.shard_map(
        on_device,
        mesh=mesh,
        in_specs=(
            P("tm", None, "space"),
            P(None, None, None, None, ("space", "tm")),
            P(),
            P(("space", "tm")),
            P(),
        ),
        out_specs=(P(), P(None, None, None, None, ("space", "tm"))),
        check_vma=False,
    )
```

time: 43.4 us -> 37.1 us (0.85)
  local copies, waits for them, and re-layouts: 6.8 us -> 2.13 us
  Pallas kernels: 35.6 us -> 34.2 us
    unnamed x12 -> x2, local copies, waits for them, and re-layouts: 6.58 us -> 1.91 us
    pallas_call x1, Pallas kernels: 35.6 us -> 34.2 us  [on_device(): pl.pallas_call(functools.partial(kernel, n_tm, n_sp, low, entries, chunks...]
where the time goes in v2:
time: 37.1 us; the launch traced here: 37 us
  Pallas kernels  34.2 us (92%)
  local copies, waits for them, and re-layouts  2.13 us (6%)
  between operations  0.66 us (2%)
    pallas_call x1, Pallas kernels, on_device(): pl.pallas_call(functools.partial(kernel, n_tm, n_sp, low, entries, chunks...  34.2 us
    unnamed x2, local copies, waits for them, and re-layouts  1.91 us

profile of v2, /device:TPU:0, one launch (start us, length us, event | category | flops | bytes accessed | tf_op | source)
XLA Modules:
  0.0 37.0 jit_solution(8902071720193245830)
XLA Ops:
  0.6 34.2 %shard_map.68 = (f32[2,5,8,128]{3,2,1,0:T(8,128)S(1)}, bf16[2,33,5,16,128]{4,3,2,1,0:T(8,128)(2,1)S(1)}) custom-call(bf16[5,32,2048]{2,1,0:T(8,128)(2,1)} %bitcast.11, bf16[2,33,5,16,128]{4,3,2,1,0:T(8,128)(2,1)} %bitcast.9, f32[8,64,64]{2,1,0:T(8,128)} %mass_in.1, s32[2]{0:T(128)} %kinds_in.1, s32[8]{0:T(128)} %offs_in.1), custom_call_target="tpu_custom_call" | custom-call | tf_op jit(solution)/shard_map/pallas_call | solution.py:301
  34.8 0.1 reshape.10
  34.9 0.1 copy.8
  35.0 0.8 %copy.9 = f32[2,33,8,16]{1,3,2,0:T(8,128)} copy(f32[2,33,8,16]{3,2,1,0:T(8,128)S(1)} %slice.4) | data formatting | bytes 67584
  35.9 1.1 %copy.11 = bf16[2,33,16,5,128]{4,2,3,1,0:T(8,128)(2,1)} copy(bf16[2,33,16,5,128]{4,2,3,1,0:T(8,128)(2,1)S(1)} %bitcast.8) | data formatting | bytes 2703360
  (1 shorter events, 0.0 us)

commit v3 on v2

--- a/solution.py
+++ b/solution.py
@@ -22,8 +22,8 @@
 def kernel(
     n_tm, n_sp, low, entries, chunks,
     snap, basis, mass_in, kinds_in, offs_in,
-    coef_out, new_out,
-    table, ub, sh, xb, line, plane, yb, mass, kinds, offs, *rest,
+    sh, y_out,
+    table, ub, xb, line, plane, yb, mass, kinds, offs, *rest,
 ):
     recs, (a_send, a_recv, l_sem, s1, r1, s2, r2, s3, r3) = rest[: len(chunks)], rest[len(chunks) :]
     tm = lax.axis_index("tm")
@@ -228,23 +228,48 @@
     def _():
         wait_bytes(yb, r3)
 
+    y_out[...] = yb[...]
+    for ci in range(len(chunks)):
+        wait_bytes(recs[ci].at[pl.ds(0, n_tm - 1)], a_send.at[ci])
+
+    @pl.when(spot < owners)
+    def _():
+        wait_bytes(xb.at[pl.ds(0, (owners - 1) * upo)], s1)
+        if high > 1:
+            wait_bytes(line.at[pl.ds(0, high - 1)], s2)
+        wait_bytes(plane.at[pl.ds(0, side - 1)], s3)
+
+    @pl.when(spot >= owners)
+    def _():
+        wait_bytes(xb, s1)
+
+
+def finish(entries, yb, sh, coef_out, new_out, ob, o_sem):
+    freqs, nvar, modes, pts = new_out.shape[1:]
+    blocks = coef_out.shape[1]
+    half = GROUP * blocks
+    lanes = GROUP * modes
+    groups = -(-freqs // GROUP)
+    row_f = lax.broadcasted_iota(jnp.int32, (GROUP, blocks, lanes), 0)
+    lane = lax.broadcasted_iota(jnp.int32, (GROUP, blocks, lanes), 2)
+    diag_k = row_f == lane // modes
+    diag_b = row_f == (lane % half) // blocks
+    lane2 = lax.broadcasted_iota(jnp.int32, (blocks, lanes), 1)
     scale = 1.0 / math.sqrt(entries)
-    nvar = sh.shape[1] // pts
+
+    def spread_rows(val, mask):
+        big = jnp.broadcast_to(val[None], (GROUP, blocks, lanes))
+        return jnp.where(mask, big, 0.0).reshape(half, lanes)
+
+    copies, held = [], []
     for g in range(groups):
         top = g * 2 * half
         f0 = g * GROUP
         nf = min(GROUP, freqs - f0)
-        co_r, co_i = yb[3 * g] * scale, yb[3 * g + 1] * scale
-        coef_out[0, g] = co_r
-        coef_out[1, g] = co_i
-        cr = co_r.astype(BF).astype(F32)
-        ci = co_i.astype(BF).astype(F32)
+        co = [yb[3 * g + c] * scale for c in range(2)]
+        held.append(co)
+        cr, ci = [v.astype(BF).astype(F32) for v in co]
         gram = yb[3 * g + 2]
-
-        def spread_rows(val, mask):
-            big = jnp.broadcast_to(val[None], (GROUP, blocks, lanes))
-            return jnp.where(mask, big, 0.0).reshape(half, lanes)
-
         d_r, d_i = spread_rows(cr, diag_k), spread_rows(ci, diag_k)
         turned = pltpu.roll(gram, half, 1)
         turned = jnp.where(lane2 < half, -turned, turned)
@@ -259,21 +284,31 @@
             field = mm(jnp.transpose(d).astype(BF), s_g, ((1,), (0,)))
             for v in range(nvar):
                 val = (field[:, v * pts : (v + 1) * pts] * fac).astype(BF).reshape(GROUP, modes, pts)
-                new_out[c, f0 : f0 + nf, v] = val[:nf]
-
-    for ci in range(len(chunks)):
-        wait_bytes(recs[ci].at[pl.ds(0, n_tm - 1)], a_send.at[ci])
-
-    @pl.when(spot < owners)
-    def _():
-        wait_bytes(xb.at[pl.ds(0, (owners - 1) * upo)], s1)
-        if high > 1:
-            wait_bytes(line.at[pl.ds(0, high - 1)], s2)
-        wait_bytes(plane.at[pl.ds(0, side - 1)], s3)
-
-    @pl.when(spot >= owners)
-    def _():
-        wait_bytes(xb, s1)
+                ob[c, f0 : f0 + nf, v] = val[:nf]
+        cp = pltpu.make_async_copy(ob.at[:, pl.ds(f0, nf)], new_out.at[:, pl.ds(f0, nf)], o_sem.at[g])
+        cp.start()
+        copies.append(cp)
+
+    mode_row = lax.broadcasted_iota(jnp.int32, (blocks, modes, lanes), 1)
+    pick = mode_row == lax.broadcasted_iota(jnp.int32, (blocks, modes, lanes), 2) % modes
+    e_row = lax.broadcasted_iota(jnp.int32, (lanes, freqs), 0) // modes
+    e_col = lax.broadcasted_iota(jnp.int32, (lanes, freqs), 1)
+    moves = [jnp.where(e_col == e_row + g * GROUP, 1.0, 0.0).astype(BF) for g in range(groups)]
+    move = jnp.concatenate(moves + moves, axis=0)
+    for c in range(2):
+        his, los = [], []
+        for g in range(groups):
+            val = held[g][c]
+            if g == groups - 1:
+                val = jnp.where(lane2 < (freqs - g * GROUP) * modes, val, 0.0)
+            hi = val.astype(BF).astype(F32)
+            for part, to in ((hi, his), (val - hi, los)):
+                big = jnp.broadcast_to(part[:, None, :], (blocks, modes, lanes))
+                to.append(jnp.where(pick, big, 0.0).reshape(blocks * modes, lanes).astype(BF))
+        moved = mm(jnp.concatenate(his + los, axis=1), move, ((1,), (0,)))
+        coef_out[c] = moved.reshape(blocks, modes, freqs)
+    for cp in copies:
+        cp.wait()
 
 
 def solution(mesh):
@@ -298,18 +333,17 @@
         base = jnp.transpose(basis, (0, 1, 3, 2, 4))
         hbm = pl.BlockSpec(memory_space=pltpu.HBM)
         vmem = pl.BlockSpec(memory_space=pltpu.VMEM)
-        coef, new = pl.pallas_call(
+        spec, total = pl.pallas_call(
             functools.partial(kernel, n_tm, n_sp, low, entries, chunks),
             out_shape=(
-                jax.ShapeDtypeStruct((2, groups, blocks, GROUP * modes), F32),
-                jax.ShapeDtypeStruct(base.shape, BF),
+                jax.ShapeDtypeStruct((table_rows, nvar * pts), BF),
+                jax.ShapeDtypeStruct((owners * upo,) + unit, F32),
             ),
             in_specs=[hbm] * 5,
             out_specs=(vmem, vmem),
             scratch_shapes=[
                 pltpu.VMEM((table_rows, rows * n_tm), BF),
                 pltpu.VMEM((2, groups * GROUP, nvar, modes, pts), BF),
-                pltpu.VMEM((table_rows, nvar * pts), BF),
                 pltpu.VMEM((owners * upo,) + unit, F32),
                 pltpu.VMEM((n_tm // low, upo) + unit, F32),
                 pltpu.VMEM((side, upo) + unit, F32),
@@ -329,9 +363,18 @@
                 collective_id=0, has_side_effects=True, vmem_limit_bytes=48 * 1024 * 1024
             ),
         )(*[pltpu.with_memory_space_constraint(a, pltpu.HBM) for a in (snap, base, mass_table, elem_kind, offsets)])
-        coef = coef.reshape(2, groups, blocks, GROUP, modes).transpose(0, 1, 3, 2, 4)
-        coef = coef.reshape(2, groups * GROUP, blocks, modes)[:, :freqs]
-        return coef, jnp.transpose(new, (0, 1, 3, 2, 4))
+        coef, new = pl.pallas_call(
+            functools.partial(finish, entries),
+            out_shape=(
+                jax.ShapeDtypeStruct((2, blocks, modes, freqs), F32),
+                jax.ShapeDtypeStruct(base.shape, BF),
+            ),
+            in_specs=[vmem, vmem],
+            out_specs=(vmem, hbm),
+            scratch_shapes=[pltpu.VMEM(base.shape, BF), pltpu.SemaphoreType.DMA((groups,))],
+            compiler_params=pltpu.CompilerParams(vmem_limit_bytes=32 * 1024 * 1024),
+        )(total, spec)
+        return jnp.transpose(coef, (0, 3, 1, 2)), jnp.transpose(new, (0, 1, 3, 2, 4))
 
     return jax.shard_map(
         on_device,

time: 37.1 us -> 36.4 us (0.981)
  local copies, waits for them, and re-layouts: 2.13 us -> 0 us
  Pallas kernels: 34.2 us -> 35.6 us
    pallas_call x0 -> x1, Pallas kernels: none -> 2.14 us  [on_device(): pl.pallas_call(functools.partial(finish, entries), out_shape=(jax.ShapeDt...]
    unnamed x2 -> x0, local copies, waits for them, and re-layouts: 1.91 us -> none
    pallas_call x1, Pallas kernels: 34.2 us -> 33.4 us  [on_device(): pl.pallas_call(functools.partial(kernel, n_tm, n_sp, low, entries, chunks...]
where the time goes in v3:
time: 36.4 us; the launch traced here: 36.2 us
  Pallas kernels  35.6 us (98%)
  between operations  0.64 us (2%)
    pallas_call x1, Pallas kernels, on_device(): pl.pallas_call(functools.partial(kernel, n_tm, n_sp, low, entries, chunks...  33.4 us
    pallas_call x1, Pallas kernels, on_device(): pl.pallas_call(functools.partial(finish, entries), out_shape=(jax.ShapeDt...  2.14 us

profile of v3, /device:TPU:0, one launch (start us, length us, event | category | flops | bytes accessed | tf_op | source)
XLA Modules:
  0.0 36.2 jit_solution(14520034552095687105)
XLA Ops:
  0.6 33.4 %shard_map.68 = (bf16[640,640]{1,0:T(8,128)(2,1)S(1)}, f32[16,8,128]{2,1,0:T(8,128)S(1)}) custom-call(bf16[5,32,2048]{2,1,0:T(8,128)(2,1)} %bitcast.5, bf16[2,33,5,16,128]{4,3,2,1,0:T(8,128)(2,1)} %bitcast.4, f32[8,64,64]{2,1,0:T(8,128)} %mass_in.1, s32[2]{0:T(128)} %kinds_in.1, s32[8]{0:T(128)} %offs_in.1), custom_call_target="tpu_custom_call" | custom-call | tf_op jit(solution)/shard_map/pallas_call | solution.py:336
  34.1 2.1 %shard_map.69 = (f32[2,8,16,33]{3,2,1,0:T(8,128)}, bf16[2,33,5,16,128]{4,3,2,1,0:T(8,128)(2,1)}) custom-call(f32[16,8,128]{2,1,0:T(8,128)S(1)} %get-tuple-element.6.yb, bf16[640,640]{1,0:T(8,128)(2,1)S(1)} %get-tuple-element.7.sh), custom_call_target="tpu_custom_call" | custom-call | tf_op jit(solution)/shard_map/pallas_call | solution.py:366

commit v4 on v3

--- a/solution.py
+++ b/solution.py
@@ -30,7 +30,9 @@
     sp = lax.axis_index("space")
     high = n_tm // low
     side = low * n_sp
-    spot = sp * low + lax.rem(tm, low)
+    mid = n_tm // 2
+    turn = lax.rem(tm + n_tm - n_tm // 4, n_tm)
+    spot = lax.div(turn, mid) * (side // 2) + sp * mid + lax.rem(turn, mid)
     level = lax.div(tm, low)
     freqs = basis.shape[1]
     rows, pts = recs[0].shape[2:]
@@ -44,7 +46,9 @@
     lanes = GROUP * modes
 
     def beside(p):
-        return {"tm": level * low + lax.rem(p, low), "space": lax.div(p, low)}
+        r = lax.rem(p, side // 2)
+        back = lax.div(p, side // 2) * mid + lax.rem(r, mid)
+        return {"tm": lax.rem(back + n_tm // 4, n_tm), "space": lax.div(r, mid)}
 
     barrier = pltpu.get_barrier_semaphore()
 
@@ -322,7 +326,7 @@
         groups = -(-freqs // GROUP)
         entries = nvar * pts * n
         units = 3 * groups
-        low = math.gcd(n_tm, 4)
+        low = n_tm
         side = low * n_sp
         upo = -(-units // side)
         owners = -(-units // upo)

time: 36.4 us -> 35.7 us (0.981)
  Pallas kernels: 35.6 us -> 34.9 us
    pallas_call x1, Pallas kernels: 33.4 us -> 32.7 us  [on_device(): pl.pallas_call(functools.partial(kernel, n_tm, n_sp, low, entries, chunks...]
where the time goes in v4:
time: 35.7 us; the launch traced here: 35.5 us
  Pallas kernels  34.9 us (98%)
  between operations  0.64 us (2%)
    pallas_call x1, Pallas kernels, on_device(): pl.pallas_call(functools.partial(kernel, n_tm, n_sp, low, entries, chunks...  32.7 us
    pallas_call x1, Pallas kernels, on_device(): pl.pallas_call(functools.partial(finish, entries), out_shape=(jax.ShapeDt...  2.14 us

profile of v4, /device:TPU:0, one launch (start us, length us, event | category | flops | bytes accessed | tf_op | source)
XLA Modules:
  0.0 35.5 jit_solution(3388554839246065321)
XLA Ops:
  0.6 32.7 %shard_map.68 = (bf16[640,640]{1,0:T(8,128)(2,1)S(1)}, f32[15,8,128]{2,1,0:T(8,128)S(1)}) custom-call(bf16[5,32,2048]{2,1,0:T(8,128)(2,1)} %bitcast.5, bf16[2,33,5,16,128]{4,3,2,1,0:T(8,128)(2,1)} %bitcast.4, f32[8,64,64]{2,1,0:T(8,128)} %mass_in.1, s32[2]{0:T(128)} %kinds_in.1, s32[8]{0:T(128)} %offs_in.1), custom_call_target="tpu_custom_call" | custom-call | tf_op jit(solution)/shard_map/pallas_call | solution.py:340
  33.4 2.1 %shard_map.69 = (f32[2,8,16,33]{3,2,1,0:T(8,128)}, bf16[2,33,5,16,128]{4,3,2,1,0:T(8,128)(2,1)}) custom-call(f32[15,8,128]{2,1,0:T(8,128)S(1)} %get-tuple-element.6.yb, bf16[640,640]{1,0:T(8,128)(2,1)S(1)} %get-tuple-element.7.sh), custom_call_target="tpu_custom_call" | custom-call | tf_op jit(solution)/shard_map/pallas_call | solution.py:370

commit v5 on v4

--- a/solution.py
+++ b/solution.py
@@ -65,8 +65,8 @@
         )
         return carry
 
-    lax.fori_loop(1, n_tm, greet_line, 0)
-    lax.fori_loop(low, side, greet_side, 0)
+    lax.fori_loop(1, n_tm, greet_line, 0, unroll=side <= 32)
+    lax.fori_loop(low, side, greet_side, 0, unroll=side <= 32)
     loads = [
         pltpu.make_async_copy(offs_in, offs, l_sem.at[0]),
         pltpu.make_async_copy(kinds_in, kinds, l_sem.at[1]),
@@ -91,7 +91,7 @@
             ).start()
             return carry
 
-        lax.fori_loop(0, n_tm - 1, send, 0)
+        lax.fori_loop(0, n_tm - 1, send, 0, unroll=side <= 32)
         pltpu.make_async_copy(block(tm), recs[ci].at[tm], a_recv.at[ci]).start()
 
     loads[0].wait()
@@ -194,7 +194,7 @@
 
         return carry
 
-    lax.fori_loop(0, owners, scatter, 0)
+    lax.fori_loop(0, owners, scatter, 0, unroll=side <= 32)
 
     def wait_bytes(ref, sem):
         pltpu.make_async_copy(ref, ref, sem).wait()
@@ -225,7 +225,7 @@
             ).start()
             return carry
 
-        lax.fori_loop(1, side, gather, 0)
+        lax.fori_loop(1, side, gather, 0, unroll=side <= 32)
         wait_bytes(yb.at[pl.ds(0, (owners - 1) * upo)], r3)
 
     @pl.when(spot >= owners)

time: 35.7 us -> 35.4 us (level)
  no operation moved by 1% of the time
where the time goes in v5:
time: 35.4 us; the launch traced here: 35.2 us
  Pallas kernels  34.6 us (98%)
  between operations  0.64 us (2%)
    pallas_call x1, Pallas kernels, on_device(): pl.pallas_call(functools.partial(kernel, n_tm, n_sp, low, entries, chunks...  32.5 us
    pallas_call x1, Pallas kernels, on_device(): pl.pallas_call(functools.partial(finish, entries), out_shape=(jax.ShapeDt...  2.14 us

profile of v5, /device:TPU:0, one launch (start us, length us, event | category | flops | bytes accessed | tf_op | source)
XLA Modules:
  0.0 35.2 jit_solution(7653104731778670101)
XLA Ops:
  0.6 32.5 %shard_map.68 = (bf16[640,640]{1,0:T(8,128)(2,1)S(1)}, f32[15,8,128]{2,1,0:T(8,128)S(1)}) custom-call(bf16[5,32,2048]{2,1,0:T(8,128)(2,1)} %bitcast.5, bf16[2,33,5,16,128]{4,3,2,1,0:T(8,128)(2,1)} %bitcast.4, f32[8,64,64]{2,1,0:T(8,128)} %mass_in.1, s32[2]{0:T(128)} %kinds_in.1, s32[8]{0:T(128)} %offs_in.1), custom_call_target="tpu_custom_call" | custom-call | tf_op jit(solution)/shard_map/pallas_call | solution.py:340
  33.1 2.1 %shard_map.69 = (f32[2,8,16,33]{3,2,1,0:T(8,128)}, bf16[2,33,5,16,128]{4,3,2,1,0:T(8,128)(2,1)}) custom-call(f32[15,8,128]{2,1,0:T(8,128)S(1)} %get-tuple-element.6.yb, bf16[640,640]{1,0:T(8,128)(2,1)S(1)} %get-tuple-element.7.sh), custom_call_target="tpu_custom_call" | custom-call | tf_op jit(solution)/shard_map/pallas_call | solution.py:370
